TPU v7x, 32 devices: a whole 2x2x4 slice. The times are simulated.
32 devices in a mesh: aux: 4 (over y, x), occ: 8 (over z, core).
Axes of the slice: x: 2, y: 2, z: 4, core: 2. Of those that a mesh axis runs over, the one named last changes fastest.
Arguments:
- three_index: bfloat16 [2048, 32, 256], P('aux', 'occ'), may hold values from -0.8984375 to 0.8984375
- pair_list: int32 [8, 6], replicated, may hold values from 0 to 7
- pair_counts: int32 [8], replicated, may hold values from 1 to 6, as said below
- domains: int32 [8, 256], replicated, may hold values from 0 to 2047
- pao_energy: float32 [2048], replicated, may hold values from 0.5 to 3
- occ_energy: float32 [32], replicated, may hold values from -2 to -0.3
Outputs:
- density: bfloat16 [2048, 32, 256], P('aux', 'occ')
- pair_energy: float32 [8, 6], P('occ')
Inputs may be any that keep to these rules, and one draw needn't show every extreme that they name: `pair_list`: slots at or past a block's count are unused. `pair_counts`: some block uses all 6 slots.
All inputs are finite; a program needn't handle non-finite values.
Results may differ from a plain program's by a relative error of at most 0.0031.
Values may be sent and summed in bfloat16 or wider, within the bound.
No kernel may reach another device: no remote copies, remote signals or barrier semaphores. Data moves between devices by JAX's collectives and lax.ppermute only.
A program may use at most 64 MiB of HBM per device.

v0:
```python
import jax
import jax.numpy as jnp
from jax import lax
from jax.sharding import PartitionSpec as P


def per_device(three_index, pair_list, pair_counts, domains, pao_energy, occ_energy):
    aux_local, occ_dev, dom_width = three_index.shape
    pair_rows = occ_dev * dom_width
    block_count = lax.axis_size("occ")
    block_id = lax.axis_index("occ")
    aux_count = lax.axis_size("aux")
    aux_rank = lax.axis_index("aux")
    share_rows = pair_rows // aux_count
    slot_total = pair_list.shape[1]
    own_block = three_index.reshape(aux_local, pair_rows)
    levels = jnp.take(pao_energy, domains, axis=0)
    occ_levels = occ_energy.reshape(block_count, occ_dev)
    denoms = (levels[:, None, :] - occ_levels[:, :, None]).reshape(block_count, pair_rows)
    own_denom = denoms[block_id]
    row_denom = lax.dynamic_slice_in_dim(own_denom, aux_rank * share_rows, share_rows, 0)
    my_pairs = pair_list[block_id]
    my_count = pair_counts[block_id]
    all_blocks = lax.all_gather(own_block[None], "occ", axis=0, tiled=True)

    def partner_of(slot_id):
        return all_blocks[my_pairs[slot_id]]

    def scaled(integrals, slot_id):
        partner_id = my_pairs[slot_id]
        slot_valid = (slot_id < my_count).astype(jnp.float32)
        amplitude = (
            integrals / (row_denom[:, None] + denoms[partner_id][None, :]) * slot_valid
        ).astype(jnp.bfloat16)
        energy_part = jnp.sum(amplitude.astype(jnp.float32) * integrals) / (pair_rows * pair_rows)
        return (amplitude, energy_part)

    energies = jnp.zeros((slot_total,), jnp.float32)

    def one_slot(slot_id, state_pair):
        density, energies = state_pair
        partner = partner_of(slot_id)
        integrals = lax.psum_scatter(
            jnp.einsum("ar,ac->rc", own_block, partner, preferred_element_type=jnp.float32),
            "aux",
            scatter_dimension=0,
            tiled=True,
        )
        amplitude, energy_part = scaled(integrals, slot_id)
        density = density + jnp.einsum(
            "ac,rc->ar",
            partner,
            lax.all_gather(amplitude, "aux", axis=0, tiled=True),
            preferred_element_type=jnp.float32,
        )
        return (density, energies.at[slot_id].set(energy_part))

    density, energies = lax.fori_loop(
        0, slot_total, one_slot, (jnp.zeros((aux_local, pair_rows), jnp.float32), energies)
    )
    density_out = density.astype(jnp.bfloat16)
    energies = lax.psum(energies, "aux")
    return (density_out.reshape(aux_local, occ_dev, dom_width), energies[None])


def solution(mesh):
    placed = (P("aux", "occ", None), P(), P(), P(), P(), P())
    return jax.shard_map(
        per_device,
        mesh=mesh,
        in_specs=placed,
        out_specs=(P("aux", "occ", None), P("occ", None)),
        check_vma=False,
    )
```

profile of v0, /device:TPU:0, one launch (start us, length us, event | category | flops | bytes accessed | tf_op | source)
XLA Modules:
  0.0 722.3 jit_solution(9689059102581887274)
XLA Ops:
  9.9 11.8 %gather_fusion = f32[2048]{0:T(1024)S(1)} fusion(f32[2048]{0:T(1024)S(1)} %copy-done, s32[2048]{0:T(1024)S(1)} %broadcast_clamp_fusion), kind=kCustom, calls=%fused_computation | custom fusion | bytes 24576 | tf_op jit(solution)/shard_map/jit(_take)/gather | solution.py:17
  24.7 70.3 %all-gather.3.cloned.1.call-done = bf16[8,512,1024]{2,1,0:T(8,128)(2,1)} async-done(((bf16[1,512,1024]{2,1,0:T(8,128)(2,1)}), bf16[8,512,1024]{2,1,0:T(8,128)(2,1)}) %all-gather.3.cloned.1.call-update) | async-done | bytes 8388624 | tf_op jit(solution)/shard_map/all_gather | solution.py:24
  95.0 609.7 %while.17 = (s32[]{:T(128)}, f32[512,1024]{1,0:T(8,128)S(1)}, f32[6]{0:T(128)S(1)}, s32[6]{0:T(128)S(1)}, bf16[8,512,1024]{2,1,0:T(8,128)(2,1)}, /*index=5*/bf16...) while((s32[]{:T(128)}, f32[512,1024]{1,0:T(8,128)S(1)}, ...), condition=%wide.region_3.4_spmd.clone, body=%wide.region_0.3_spmd.clone.sunk | while | flops 2150367232 | bytes 38811020 | solution.py:58
  97.5 4.8 convolution_bitcast_fusion.2
  103.0 50.6 %reduce-scatter.2.cloned.1.call-done = f32[256,1024]{0,1:T(8,128)} async-done(((f32[1024,1024]{0,1:T(8,128)}), f32[256,1024]{0,1:T(8,128)}) %reduce-scatter.2.cloned.1.call-update) | async-done | bytes 1048592 | tf_op jit(solution)/shard_map/while/body/eval_jaxpr/reduce_scatter | solution.py:43
  153.6 3.0 multiply_reduce_fusion.2
  157.4 34.3 %all-gather.5.cloned.1.call-done = bf16[1024,1024]{0,1:T(8,128)(2,1)} async-done(((bf16[256,1024]{0,1:T(8,128)(2,1)}), bf16[1024,1024]{0,1:T(8,128)(2,1)}) %all-gather.5.cloned.1.call-update) | async-done | bytes 2097168 | tf_op jit(solution)/shard_map/while/body/eval_jaxpr/all_gather | solution.py:53
  191.8 3.5 select_add_fusion.2
  197.9 4.8 convolution_bitcast_fusion.2
  203.4 52.1 %reduce-scatter.2.cloned.1.call-done = f32[256,1024]{0,1:T(8,128)} async-done(((f32[1024,1024]{0,1:T(8,128)}), f32[256,1024]{0,1:T(8,128)}) %reduce-scatter.2.cloned.1.call-update) | async-done | bytes 1048592 | tf_op jit(solution)/shard_map/while/body/eval_jaxpr/reduce_scatter | solution.py:43
  255.4 3.0 multiply_reduce_fusion.2
  259.3 34.3 %all-gather.5.cloned.1.call-done = bf16[1024,1024]{0,1:T(8,128)(2,1)} async-done(((bf16[256,1024]{0,1:T(8,128)(2,1)}), bf16[1024,1024]{0,1:T(8,128)(2,1)}) %all-gather.5.cloned.1.call-update) | async-done | bytes 2097168 | tf_op jit(solution)/shard_map/while/body/eval_jaxpr/all_gather | solution.py:53
  293.6 3.5 select_add_fusion.2
  299.7 4.8 convolution_bitcast_fusion.2
  305.2 52.1 %reduce-scatter.2.cloned.1.call-done = f32[256,1024]{0,1:T(8,128)} async-done(((f32[1024,1024]{0,1:T(8,128)}), f32[256,1024]{0,1:T(8,128)}) %reduce-scatter.2.cloned.1.call-update) | async-done | bytes 1048592 | tf_op jit(solution)/shard_map/while/body/eval_jaxpr/reduce_scatter | solution.py:43
  357.3 3.0 multiply_reduce_fusion.2
  361.2 34.3 %all-gather.5.cloned.1.call-done = bf16[1024,1024]{0,1:T(8,128)(2,1)} async-done(((bf16[256,1024]{0,1:T(8,128)(2,1)}), bf16[1024,1024]{0,1:T(8,128)(2,1)}) %all-gather.5.cloned.1.call-update) | async-done | bytes 2097168 | tf_op jit(solution)/shard_map/while/body/eval_jaxpr/all_gather | solution.py:53
  395.5 3.5 select_add_fusion.2
  401.6 4.8 convolution_bitcast_fusion.2
  407.1 52.1 %reduce-scatter.2.cloned.1.call-done = f32[256,1024]{0,1:T(8,128)} async-done(((f32[1024,1024]{0,1:T(8,128)}), f32[256,1024]{0,1:T(8,128)}) %reduce-scatter.2.cloned.1.call-update) | async-done | bytes 1048592 | tf_op jit(solution)/shard_map/while/body/eval_jaxpr/reduce_scatter | solution.py:43
  459.2 3.0 multiply_reduce_fusion.2
  463.0 34.3 %all-gather.5.cloned.1.call-done = bf16[1024,1024]{0,1:T(8,128)(2,1)} async-done(((bf16[256,1024]{0,1:T(8,128)(2,1)}), bf16[1024,1024]{0,1:T(8,128)(2,1)}) %all-gather.5.cloned.1.call-update) | async-done | bytes 2097168 | tf_op jit(solution)/shard_map/while/body/eval_jaxpr/all_gather | solution.py:53
  497.4 3.5 select_add_fusion.2
  503.5 4.8 convolution_bitcast_fusion.2
  509.0 52.1 %reduce-scatter.2.cloned.1.call-done = f32[256,1024]{0,1:T(8,128)} async-done(((f32[1024,1024]{0,1:T(8,128)}), f32[256,1024]{0,1:T(8,128)}) %reduce-scatter.2.cloned.1.call-update) | async-done | bytes 1048592 | tf_op jit(solution)/shard_map/while/body/eval_jaxpr/reduce_scatter | solution.py:43
  564.9 34.3 %all-gather.5.cloned.1.call-done = bf16[1024,1024]{0,1:T(8,128)(2,1)} async-done(((bf16[256,1024]{0,1:T(8,128)(2,1)}), bf16[1024,1024]{0,1:T(8,128)(2,1)}) %all-gather.5.cloned.1.call-update) | async-done | bytes 2097168 | tf_op jit(solution)/shard_map/while/body/eval_jaxpr/all_gather | solution.py:53
  599.2 3.5 select_add_fusion.2
  605.4 4.8 convolution_bitcast_fusion.2
  610.9 52.1 %reduce-scatter.2.cloned.1.call-done = f32[256,1024]{0,1:T(8,128)} async-done(((f32[1024,1024]{0,1:T(8,128)}), f32[256,1024]{0,1:T(8,128)}) %reduce-scatter.2.cloned.1.call-update) | async-done | bytes 1048592 | tf_op jit(solution)/shard_map/while/body/eval_jaxpr/reduce_scatter | solution.py:43
  666.8 34.3 %all-gather.5.cloned.1.call-done = bf16[1024,1024]{0,1:T(8,128)(2,1)} async-done(((bf16[256,1024]{0,1:T(8,128)(2,1)}), bf16[1024,1024]{0,1:T(8,128)(2,1)}) %all-gather.5.cloned.1.call-update) | async-done | bytes 2097168 | tf_op jit(solution)/shard_map/while/body/eval_jaxpr/all_gather | solution.py:53
  701.1 3.5 select_add_fusion.2
  706.4 9.4 %psum.7 = f32[1,6]{1,0:T(1,128)} all-reduce(f32[1,6]{1,0:T(1,128)S(1)} %bitcast.49), channel_id=1, replica_groups=mesh['aux'=4,'occ'=8] {'aux'}, use_global_device_ids=true, to_apply=%region_4.5 | all-reduce | flops 6 | bytes 48 | tf_op jit(solution)/shard_map/psum | solution.py:62
  (73 shorter events, 18.6 us)
Async XLA Ops:
  7.2 2.7 copy-start
  7.2 2.7 copy-start.2
  7.2 87.8 %all-gather.3.cloned.1.call-start = ((), (), s32[]{:S(2)}) async-start(), calls=%async_computation.1 | async-start | bytes 9437184 | tf_op jit(solution)/shard_map/all_gather | solution.py:24
  9.9 11.8 %copy-start.3 = (f32[32]{0:T(128)S(1)}, f32[32]{0:T(128)}, u32[]{:S(2)}) copy-start(f32[32]{0:T(128)} %param.15) | copy-start | bytes 388
  9.9 12.0 %copy-start.4 = (s32[8]{0:T(128)S(1)}, s32[8]{0:T(128)}, u32[]{:S(2)}) copy-start(s32[8]{0:T(128)} %param.12) | copy-start | bytes 100
  9.9 12.6 %copy-start.1 = (bf16[512,4,256]{2,1,0:T(4,128)(2,1)S(1)}, bf16[512,4,256]{2,1,0:T(4,128)(2,1)}, u32[]{:S(2)}) copy-start(bf16[512,4,256]{2,1,0:T(4,128)(2,1)} %param.10) | copy-start | bytes 3145732
  95.0 58.6 %reduce-scatter.2.cloned.1.call-start = ((), (), s32[]{:S(2)}) async-start(), calls=%async_computation.2 | async-start | bytes 5242880 | tf_op jit(solution)/shard_map/while/body/eval_jaxpr/reduce_scatter | solution.py:43
  102.3 89.5 %all-gather.5.cloned.1.call-start = ((), (), s32[]{:S(2)}) async-start(), calls=%async_computation.3 | async-start | bytes 2621440 | tf_op jit(solution)/shard_map/while/body/eval_jaxpr/all_gather | solution.py:53
  195.3 60.1 %reduce-scatter.2.cloned.1.call-start = ((), (), s32[]{:S(2)}) async-start(), calls=%async_computation.2 | async-start | bytes 5242880 | tf_op jit(solution)/shard_map/while/body/eval_jaxpr/reduce_scatter | solution.py:43
  202.7 90.9 %all-gather.5.cloned.1.call-start = ((), (), s32[]{:S(2)}) async-start(), calls=%async_computation.3 | async-start | bytes 2621440 | tf_op jit(solution)/shard_map/while/body/eval_jaxpr/all_gather | solution.py:53
  297.2 60.1 %reduce-scatter.2.cloned.1.call-start = ((), (), s32[]{:S(2)}) async-start(), calls=%async_computation.2 | async-start | bytes 5242880 | tf_op jit(solution)/shard_map/while/body/eval_jaxpr/reduce_scatter | solution.py:43
  304.6 90.9 %all-gather.5.cloned.1.call-start = ((), (), s32[]{:S(2)}) async-start(), calls=%async_computation.3 | async-start | bytes 2621440 | tf_op jit(solution)/shard_map/while/body/eval_jaxpr/all_gather | solution.py:53
  399.0 60.1 %reduce-scatter.2.cloned.1.call-start = ((), (), s32[]{:S(2)}) async-start(), calls=%async_computation.2 | async-start | bytes 5242880 | tf_op jit(solution)/shard_map/while/body/eval_jaxpr/reduce_scatter | solution.py:43
  406.4 90.9 %all-gather.5.cloned.1.call-start = ((), (), s32[]{:S(2)}) async-start(), calls=%async_computation.3 | async-start | bytes 2621440 | tf_op jit(solution)/shard_map/while/body/eval_jaxpr/all_gather | solution.py:53
  500.9 60.1 %reduce-scatter.2.cloned.1.call-start = ((), (), s32[]{:S(2)}) async-start(), calls=%async_computation.2 | async-start | bytes 5242880 | tf_op jit(solution)/shard_map/while/body/eval_jaxpr/reduce_scatter | solution.py:43
  508.3 90.9 %all-gather.5.cloned.1.call-start = ((), (), s32[]{:S(2)}) async-start(), calls=%async_computation.3 | async-start | bytes 2621440 | tf_op jit(solution)/shard_map/while/body/eval_jaxpr/all_gather | solution.py:53
  602.8 60.1 %reduce-scatter.2.cloned.1.call-start = ((), (), s32[]{:S(2)}) async-start(), calls=%async_computation.2 | async-start | bytes 5242880 | tf_op jit(solution)/shard_map/while/body/eval_jaxpr/reduce_scatter | solution.py:43
  610.2 90.9 %all-gather.5.cloned.1.call-start = ((), (), s32[]{:S(2)}) async-start(), calls=%async_computation.3 | async-start | bytes 2621440 | tf_op jit(solution)/shard_map/while/body/eval_jaxpr/all_gather | solution.py:53
Sparse Core Ops, SparseCore 0:
  10.2 84.7 all-gather.2
  102.4 51.0 reduce-scatter.1
  156.7 35.0 all-gather.4
  202.8 52.5 reduce-scatter.1
  258.6 35.0 all-gather.4
  304.7 52.5 reduce-scatter.1
  360.4 35.0 all-gather.4
  406.6 52.5 reduce-scatter.1
  462.3 35.0 all-gather.4
  508.4 52.5 reduce-scatter.1
  564.2 35.0 all-gather.4
  610.3 52.5 reduce-scatter.1
  666.0 35.0 all-gather.4
where the time goes:
time: 723 us; the launch traced here: 722 us
  waiting for transfers between devices  587 us (81%)
  matrix products  49.8 us (7%)
  local copies, waits for them, and re-layouts  22.4 us (3%)
  loops' own time  19.9 us (3%)
  other arithmetic  19.2 us (3%)
  between operations  13.9 us (2%)
  blocking collectives  9.41 us (1%)
    reduce_scatter x6, waiting for transfers between devices, one_slot(): lax.psum_scatter(jnp.einsum('ar,ac->rc', own_block, partner, preferred_el...  311 us
    all_gather x6, waiting for transfers between devices, one_slot(): lax.all_gather(amplitude, 'aux', axis=0, tiled=True)  206 us
    all_gather x1, waiting for transfers between devices, per_device(): all_blocks = lax.all_gather(own_block[None], 'occ', axis=0, tiled=True)  70.3 us
    dot_general x6, matrix products, one_slot(): jnp.einsum('ar,ac->rc', own_block, partner, preferred_element_type=jnp.fl...  28.8 us
    dot_general x6, matrix products, one_slot(): jnp.einsum('ac,rc->ar', partner, lax.all_gather(amplitude, 'aux', axis=0,...  21 us
    another operation x1, loops' own time, per_device(): lax.fori_loop(0, slot_total, one_slot, (jnp.zeros((aux_local, pair_rows),...  19.9 us
    reduce_sum x6, other arithmetic, scaled(): jnp.sum(amplitude.astype(jnp.float32) * integrals) / (pair_rows * pair_rows)  17.9 us
  transfers between devices with their start and end apart: 13, of which 13 were waited for; matrix products, arithmetic and copies ran while one was open for 2% of the time, Pallas kernels for 0%

commit v1 on v0

--- a/solution.py
+++ b/solution.py
@@ -2,6 +2,11 @@
 import jax.numpy as jnp
 from jax import lax
 from jax.sharding import PartitionSpec as P
+
+
+def all_by_exchange(x, axis, d):
+    repeated = jnp.stack([x] * lax.axis_size(axis))
+    return jnp.concatenate(lax.all_to_all(repeated, axis, 0, 0), axis=d)
 
 
 def per_device(three_index, pair_list, pair_counts, domains, pao_energy, occ_energy):
@@ -50,7 +55,7 @@
         density = density + jnp.einsum(
             "ac,rc->ar",
             partner,
-            lax.all_gather(amplitude, "aux", axis=0, tiled=True),
+            all_by_exchange(amplitude, "aux", 0),
             preferred_element_type=jnp.float32,
         )
         return (density, energies.at[slot_id].set(energy_part))

time: 723 us -> 696 us (0.963)
  waiting for transfers between devices: 587 us -> 527 us
  starting transfers between devices: 0.51 us -> 21.7 us
  local copies, waits for them, and re-layouts: 22.4 us -> 32.3 us
    all_gather x6 -> x0, waiting for transfers between devices: 206 us -> none  [one_slot(): lax.all_gather(amplitude, 'aux', axis=0, tiled=True)]
    all_to_all x0 -> x6, waiting for transfers between devices: none -> 145 us  [all_by_exchange(): return jnp.concatenate(lax.all_to_all(repeated, axis, 0, 0), axis=d)]
    all_to_all x0 -> x6, starting transfers between devices: none -> 21.6 us  [all_by_exchange(): return jnp.concatenate(lax.all_to_all(repeated, axis, 0, 0), axis=d)]
    another operation x1 -> x7, local copies, waits for them, and re-layouts: 0.01 us -> 9.72 us  [the longest x6 9.72 us: all_by_exchange(): repeated = jnp.stack([x] * lax.axis_size(axis))]
where the time goes in v1:
time: 696 us; the launch traced here: 694 us
  waiting for transfers between devices  527 us (76%)
  matrix products  53.5 us (8%)
  local copies, waits for them, and re-layouts  32.3 us (5%)
  starting transfers between devices  21.7 us (3%)
  loops' own time  20 us (3%)
  other arithmetic  16.4 us (2%)
  between operations  14.2 us (2%)
  blocking collectives  9.36 us (1%)
    reduce_scatter x6, waiting for transfers between devices, one_slot(): lax.psum_scatter(jnp.einsum('ar,ac->rc', own_block, partner, preferred_el...  311 us
    all_to_all x6, waiting for transfers between devices, all_by_exchange(): return jnp.concatenate(lax.all_to_all(repeated, axis, 0, 0), axis=d)  145 us
    all_gather x1, waiting for transfers between devices, per_device(): all_blocks = lax.all_gather(own_block[None], 'occ', axis=0, tiled=True)  71.3 us
    dot_general x6, matrix products, one_slot(): jnp.einsum('ar,ac->rc', own_block, partner, preferred_element_type=jnp.fl...  27 us
    dot_general x6, matrix products, one_slot(): jnp.einsum('ac,rc->ar', partner, all_by_exchange(amplitude, 'aux', 0), pr...  26.6 us
    all_to_all x6, starting transfers between devices, all_by_exchange(): return jnp.concatenate(lax.all_to_all(repeated, axis, 0, 0), axis=d)  21.6 us
    another operation x1, loops' own time, per_device(): lax.fori_loop(0, slot_total, one_slot, (jnp.zeros((aux_local, pair_rows),...  20 us
  transfers between devices with their start and end apart: 13, of which 13 were waited for; matrix products, arithmetic and copies ran while one was open for 2% of the time, Pallas kernels for 0%

profile of v1, /device:TPU:0, one launch (start us, length us, event | category | flops | bytes accessed | tf_op | source)
XLA Modules:
  0.0 694.3 jit_solution(16731162109898205058)
XLA Ops:
  9.9 11.8 %gather_fusion = f32[2048]{0:T(1024)S(1)} fusion(f32[2048]{0:T(1024)S(1)} %copy-done, s32[2048]{0:T(1024)S(1)} %broadcast_clamp_fusion), kind=kCustom, calls=%fused_computation | custom fusion | bytes 24576 | tf_op jit(solution)/shard_map/jit(_take)/gather | solution.py:22
  23.7 71.3 %all-gather.2.cloned.1.call-done = bf16[8,512,1024]{2,1,0:T(8,128)(2,1)} async-done(((bf16[1,512,1024]{2,1,0:T(8,128)(2,1)}), bf16[8,512,1024]{2,1,0:T(8,128)(2,1)}) %all-gather.2.cloned.1.call-update) | async-done | bytes 8388624 | tf_op jit(solution)/shard_map/all_gather | solution.py:29
  95.0 579.8 %while.17 = (s32[]{:T(128)}, f32[512,1024]{1,0:T(8,128)}, f32[6]{0:T(128)S(1)}, s32[6]{0:T(128)S(1)}, bf16[8,512,1024]{2,1,0:T(8,128)(2,1)}, /*index=5*/bf16[512...) while((s32[]{:T(128)}, f32[512,1024]{1,0:T(8,128)}, ...), condition=%wide.region_3.4_spmd.clone, body=%wide.region_0.3_spmd.clone.sunk | while | flops 2150367232 | bytes 40908164 | solution.py:63
  97.5 4.5 convolution_bitcast_fusion.2
  102.7 50.5 %reduce-scatter.2.cloned.1.call-done = f32[256,1024]{0,1:T(8,128)} async-done(((f32[1024,1024]{0,1:T(8,128)}), f32[256,1024]{0,1:T(8,128)}) %reduce-scatter.2.cloned.1.call-update) | async-done | bytes 1048592 | tf_op jit(solution)/shard_map/while/body/eval_jaxpr/reduce_scatter | solution.py:48
  157.4 3.6 all-to-all-start
  161.8 24.1 %all-to-all-done = bf16[4,256,1024]{2,1,0:T(8,128)(2,1)S(1)} async-done(((bf16[4,256,1024]{2,1,0:T(8,128)(2,1)}), bf16[4,256,1024]{2,1,0:T(8,128)(2,1)S(1)}, u32[]{:S(2)}, u32[]{:S(2)}) %all-to-all-start) | async-done | bytes 2097184 | tf_op jit(solution)/shard_map/while/body/eval_jaxpr/all_to_all | solution.py:9
  185.9 3.8 select_add_fusion.2
  192.3 4.5 convolution_bitcast_fusion.2
  197.5 52.1 %reduce-scatter.2.cloned.1.call-done = f32[256,1024]{0,1:T(8,128)} async-done(((f32[1024,1024]{0,1:T(8,128)}), f32[256,1024]{0,1:T(8,128)}) %reduce-scatter.2.cloned.1.call-update) | async-done | bytes 1048592 | tf_op jit(solution)/shard_map/while/body/eval_jaxpr/reduce_scatter | solution.py:48
  253.7 3.6 all-to-all-start
  258.1 24.1 %all-to-all-done = bf16[4,256,1024]{2,1,0:T(8,128)(2,1)S(1)} async-done(((bf16[4,256,1024]{2,1,0:T(8,128)(2,1)}), bf16[4,256,1024]{2,1,0:T(8,128)(2,1)S(1)}, u32[]{:S(2)}, u32[]{:S(2)}) %all-to-all-start) | async-done | bytes 2097184 | tf_op jit(solution)/shard_map/while/body/eval_jaxpr/all_to_all | solution.py:9
  282.2 4.5 select_add_fusion.2
  289.3 4.5 convolution_bitcast_fusion.2
  294.5 52.1 %reduce-scatter.2.cloned.1.call-done = f32[256,1024]{0,1:T(8,128)} async-done(((f32[1024,1024]{0,1:T(8,128)}), f32[256,1024]{0,1:T(8,128)}) %reduce-scatter.2.cloned.1.call-update) | async-done | bytes 1048592 | tf_op jit(solution)/shard_map/while/body/eval_jaxpr/reduce_scatter | solution.py:48
  350.7 3.6 all-to-all-start
  355.1 24.1 %all-to-all-done = bf16[4,256,1024]{2,1,0:T(8,128)(2,1)S(1)} async-done(((bf16[4,256,1024]{2,1,0:T(8,128)(2,1)}), bf16[4,256,1024]{2,1,0:T(8,128)(2,1)S(1)}, u32[]{:S(2)}, u32[]{:S(2)}) %all-to-all-start) | async-done | bytes 2097184 | tf_op jit(solution)/shard_map/while/body/eval_jaxpr/all_to_all | solution.py:9
  379.2 4.5 select_add_fusion.2
  386.3 4.5 convolution_bitcast_fusion.2
  391.5 52.1 %reduce-scatter.2.cloned.1.call-done = f32[256,1024]{0,1:T(8,128)} async-done(((f32[1024,1024]{0,1:T(8,128)}), f32[256,1024]{0,1:T(8,128)}) %reduce-scatter.2.cloned.1.call-update) | async-done | bytes 1048592 | tf_op jit(solution)/shard_map/while/body/eval_jaxpr/reduce_scatter | solution.py:48
  447.6 3.6 all-to-all-start
  452.1 24.1 %all-to-all-done = bf16[4,256,1024]{2,1,0:T(8,128)(2,1)S(1)} async-done(((bf16[4,256,1024]{2,1,0:T(8,128)(2,1)}), bf16[4,256,1024]{2,1,0:T(8,128)(2,1)S(1)}, u32[]{:S(2)}, u32[]{:S(2)}) %all-to-all-start) | async-done | bytes 2097184 | tf_op jit(solution)/shard_map/while/body/eval_jaxpr/all_to_all | solution.py:9
  476.2 4.5 select_add_fusion.2
  483.3 4.5 convolution_bitcast_fusion.2
  488.5 52.0 %reduce-scatter.2.cloned.1.call-done = f32[256,1024]{0,1:T(8,128)} async-done(((f32[1024,1024]{0,1:T(8,128)}), f32[256,1024]{0,1:T(8,128)}) %reduce-scatter.2.cloned.1.call-update) | async-done | bytes 1048592 | tf_op jit(solution)/shard_map/while/body/eval_jaxpr/reduce_scatter | solution.py:48
  549.1 24.1 %all-to-all-done = bf16[4,256,1024]{2,1,0:T(8,128)(2,1)S(1)} async-done(((bf16[4,256,1024]{2,1,0:T(8,128)(2,1)}), bf16[4,256,1024]{2,1,0:T(8,128)(2,1)S(1)}, u32[]{:S(2)}, u32[]{:S(2)}) %all-to-all-start) | async-done | bytes 2097184 | tf_op jit(solution)/shard_map/while/body/eval_jaxpr/all_to_all | solution.py:9
  573.2 4.5 select_add_fusion.2
  580.2 4.5 convolution_bitcast_fusion.2
  585.5 52.1 %reduce-scatter.2.cloned.1.call-done = f32[256,1024]{0,1:T(8,128)} async-done(((f32[1024,1024]{0,1:T(8,128)}), f32[256,1024]{0,1:T(8,128)}) %reduce-scatter.2.cloned.1.call-update) | async-done | bytes 1048592 | tf_op jit(solution)/shard_map/while/body/eval_jaxpr/reduce_scatter | solution.py:48
  646.1 24.1 %all-to-all-done = bf16[4,256,1024]{2,1,0:T(8,128)(2,1)S(1)} async-done(((bf16[4,256,1024]{2,1,0:T(8,128)(2,1)}), bf16[4,256,1024]{2,1,0:T(8,128)(2,1)S(1)}, u32[]{:S(2)}, u32[]{:S(2)}) %all-to-all-start) | async-done | bytes 2097184 | tf_op jit(solution)/shard_map/while/body/eval_jaxpr/all_to_all | solution.py:9
  670.2 4.5 select_add_fusion.2
  678.1 9.4 %psum.7 = f32[1,6]{1,0:T(1,128)} all-reduce(f32[1,6]{1,0:T(1,128)S(1)} %bitcast.53), channel_id=1, replica_groups=mesh['aux'=4,'occ'=8] {'aux'}, use_global_device_ids=true, to_apply=%region_4.5 | all-reduce | flops 6 | bytes 48 | tf_op jit(solution)/shard_map/psum | solution.py:67
  (79 shorter events, 44.3 us)
Async XLA Ops:
  7.2 2.7 copy-start
  7.2 2.7 copy-start.2
  7.2 87.8 %all-gather.2.cloned.1.call-start = ((), (), s32[]{:S(2)}) async-start(), calls=%async_computation.2 | async-start | bytes 9437184 | tf_op jit(solution)/shard_map/all_gather | solution.py:29
  9.9 11.8 %copy-start.3 = (f32[32]{0:T(128)S(1)}, f32[32]{0:T(128)}, u32[]{:S(2)}) copy-start(f32[32]{0:T(128)} %param.15) | copy-start | bytes 388
  9.9 12.0 %copy-start.4 = (s32[8]{0:T(128)S(1)}, s32[8]{0:T(128)}, u32[]{:S(2)}) copy-start(s32[8]{0:T(128)} %param.12) | copy-start | bytes 100
  9.9 12.7 %copy-start.1 = (bf16[512,4,256]{2,1,0:T(4,128)(2,1)S(1)}, bf16[512,4,256]{2,1,0:T(4,128)(2,1)}, u32[]{:S(2)}) copy-start(bf16[512,4,256]{2,1,0:T(4,128)(2,1)} %param.10) | copy-start | bytes 3145732
  95.0 58.3 %reduce-scatter.2.cloned.1.call-start = ((), (), s32[]{:S(2)}) async-start(), calls=%async_computation.3 | async-start | bytes 5242880 | tf_op jit(solution)/shard_map/while/body/eval_jaxpr/reduce_scatter | solution.py:48
  157.4 28.6 %all-to-all-start = ((bf16[4,256,1024]{2,1,0:T(8,128)(2,1)}), bf16[4,256,1024]{2,1,0:T(8,128)(2,1)S(1)}, u32[]{:S(2)}, u32[]{:S(2)}) async-start(bf16[4,256,1024]{2,1,0:T(8,128)(2,1)} %stack.13), calls=%async_computation.1 | async-start | bytes 4194304 | tf_op jit(solution)/shard_map/while/body/eval_jaxpr/all_to_all | solution.py:9
  189.8 59.8 %reduce-scatter.2.cloned.1.call-start = ((), (), s32[]{:S(2)}) async-start(), calls=%async_computation.3 | async-start | bytes 5242880 | tf_op jit(solution)/shard_map/while/body/eval_jaxpr/reduce_scatter | solution.py:48
  253.7 28.6 %all-to-all-start = ((bf16[4,256,1024]{2,1,0:T(8,128)(2,1)}), bf16[4,256,1024]{2,1,0:T(8,128)(2,1)S(1)}, u32[]{:S(2)}, u32[]{:S(2)}) async-start(bf16[4,256,1024]{2,1,0:T(8,128)(2,1)} %stack.13), calls=%async_computation.1 | async-start | bytes 4194304 | tf_op jit(solution)/shard_map/while/body/eval_jaxpr/all_to_all | solution.py:9
  286.8 59.8 %reduce-scatter.2.cloned.1.call-start = ((), (), s32[]{:S(2)}) async-start(), calls=%async_computation.3 | async-start | bytes 5242880 | tf_op jit(solution)/shard_map/while/body/eval_jaxpr/reduce_scatter | solution.py:48
  350.7 28.5 %all-to-all-start = ((bf16[4,256,1024]{2,1,0:T(8,128)(2,1)}), bf16[4,256,1024]{2,1,0:T(8,128)(2,1)S(1)}, u32[]{:S(2)}, u32[]{:S(2)}) async-start(bf16[4,256,1024]{2,1,0:T(8,128)(2,1)} %stack.13), calls=%async_computation.1 | async-start | bytes 4194304 | tf_op jit(solution)/shard_map/while/body/eval_jaxpr/all_to_all | solution.py:9
  383.7 59.8 %reduce-scatter.2.cloned.1.call-start = ((), (), s32[]{:S(2)}) async-start(), calls=%async_computation.3 | async-start | bytes 5242880 | tf_op jit(solution)/shard_map/while/body/eval_jaxpr/reduce_scatter | solution.py:48
  447.6 28.6 %all-to-all-start = ((bf16[4,256,1024]{2,1,0:T(8,128)(2,1)}), bf16[4,256,1024]{2,1,0:T(8,128)(2,1)S(1)}, u32[]{:S(2)}, u32[]{:S(2)}) async-start(bf16[4,256,1024]{2,1,0:T(8,128)(2,1)} %stack.13), calls=%async_computation.1 | async-start | bytes 4194304 | tf_op jit(solution)/shard_map/while/body/eval_jaxpr/all_to_all | solution.py:9
  480.8 59.8 %reduce-scatter.2.cloned.1.call-start = ((), (), s32[]{:S(2)}) async-start(), calls=%async_computation.3 | async-start | bytes 5242880 | tf_op jit(solution)/shard_map/while/body/eval_jaxpr/reduce_scatter | solution.py:48
  544.6 28.5 %all-to-all-start = ((bf16[4,256,1024]{2,1,0:T(8,128)(2,1)}), bf16[4,256,1024]{2,1,0:T(8,128)(2,1)S(1)}, u32[]{:S(2)}, u32[]{:S(2)}) async-start(bf16[4,256,1024]{2,1,0:T(8,128)(2,1)} %stack.13), calls=%async_computation.1 | async-start | bytes 4194304 | tf_op jit(solution)/shard_map/while/body/eval_jaxpr/all_to_all | solution.py:9
  577.7 59.8 %reduce-scatter.2.cloned.1.call-start = ((), (), s32[]{:S(2)}) async-start(), calls=%async_computation.3 | async-start | bytes 5242880 | tf_op jit(solution)/shard_map/while/body/eval_jaxpr/reduce_scatter | solution.py:48
  641.6 28.6 %all-to-all-start = ((bf16[4,256,1024]{2,1,0:T(8,128)(2,1)}), bf16[4,256,1024]{2,1,0:T(8,128)(2,1)S(1)}, u32[]{:S(2)}, u32[]{:S(2)}) async-start(bf16[4,256,1024]{2,1,0:T(8,128)(2,1)} %stack.13), calls=%async_computation.1 | async-start | bytes 4194304 | tf_op jit(solution)/shard_map/while/body/eval_jaxpr/all_to_all | solution.py:9
Sparse Core Ops, SparseCore 0:
  10.2 84.7 all-gather.1
  102.1 51.0 reduce-scatter.1
  196.9 52.5 reduce-scatter.1
  293.9 52.5 reduce-scatter.1
  390.9 52.5 reduce-scatter.1
  487.9 52.5 reduce-scatter.1
  584.9 52.5 reduce-scatter.1
